TPU v7x, 32 devices: a whole 2x2x4 slice. The times are simulated.
32 devices in a mesh: dp: 4 (over y, core), tensor: 8 (over z, x).
Axes of the slice: x: 2, y: 2, z: 4, core: 2. Of those that a mesh axis runs over, the one named last changes fastest.
Arguments:
- inputs: bfloat16 [16384, 28672], P('dp', 'tensor'), may hold values from -6 to 6
- out_grads: bfloat16 [16384, 8192], P('dp', 'tensor'), may hold values from -6 to 6
- proj_in: bfloat16 [28672, 64], P('tensor'), may hold values from -0.03125 to 0.03125
- proj_out: bfloat16 [8192, 64], P('tensor'), may hold values from -0.0625 to 0.0625
- lengths: int32 [16], replicated, may hold values from 1 to 4096, 16384 in all
- valid_feats: bfloat16 [4096, 4096], P('dp', 'tensor'), may hold values from -6 to 6
Outputs:
- scores: float32 [16, 4096], P(None, ('dp', 'tensor'))
Inputs may be any that keep to these rules, and one draw needn't show every extreme that they name: The lengths sum to 16384; the largest is exactly 4096.
All inputs are finite; a program needn't handle non-finite values.
Results may differ from a plain program's by a relative error of at most 0.003.
Values sent between devices are 32-bit elements; how exact they have to be, the bound alone decides.
No kernel may reach another device: no remote copies, remote signals or barrier semaphores. Data moves between devices by JAX's collectives and lax.ppermute only.
A program may use at most 128 MiB of HBM per device.

v0:
```python
import jax
import jax.numpy as jnp
from jax import lax
from jax.sharding import PartitionSpec as P


def member_rows(positions, prompt_starts, prompt_ends):
    inside = (positions[None, :] >= prompt_starts[:, None]) & (
        positions[None, :] < prompt_ends[:, None]
    )
    return inside.astype(jnp.float32)


def outer_sums(members, grad_rows, act_rows):
    return jnp.einsum(
        "pt,ti,tj->pij", members, grad_rows, act_rows, precision=lax.Precision.HIGHEST
    )


def shards(inputs, out_grads, proj_in, proj_out, lengths, valid_feats):
    tok_rows = inputs.shape[0]
    proj_rank = proj_in.shape[1]
    prompt_count = lengths.shape[0]
    act_part = jnp.dot(inputs, proj_in, preferred_element_type=jnp.float32)
    grad_part = jnp.dot(out_grads, proj_out, preferred_element_type=jnp.float32)
    paired = jnp.concatenate([act_part, grad_part], axis=1)
    prompt_ends = jnp.cumsum(lengths)
    prompt_starts = prompt_ends - lengths
    tensor_count = lax.axis_size("tensor")
    tensor_pos = lax.axis_index("tensor")
    slice_width = proj_rank * proj_rank // tensor_count
    first_row = lax.axis_index("dp") * tok_rows
    summed_pair = lax.psum(paired, "tensor")
    row_count = proj_rank // tensor_count
    grad_rows = lax.dynamic_slice_in_dim(
        summed_pair[:, proj_rank:], tensor_pos * row_count, row_count, 1
    )
    positions = first_row + jnp.arange(tok_rows, dtype=jnp.int32)
    members = member_rows(positions, prompt_starts, prompt_ends)
    gram_rows = outer_sums(members, grad_rows, summed_pair[:, :proj_rank])
    gram_rows = gram_rows.reshape(prompt_count, slice_width)
    summed = lax.psum(gram_rows, "dp")
    features = (summed / lengths[:, None].astype(jnp.float32)).astype(jnp.bfloat16)
    partial_value = lax.dot_general(
        features, valid_feats, (((1,), (1,)), ((), ())), preferred_element_type=jnp.float32
    )
    return lax.psum_scatter(partial_value, "tensor", scatter_dimension=1, tiled=True)


def solution(mesh):
    return jax.shard_map(
        shards,
        mesh=mesh,
        in_specs=(
            P("dp", "tensor"),
            P("dp", "tensor"),
            P("tensor", None),
            P("tensor", None),
            P(),
            P("dp", "tensor"),
        ),
        out_specs=P(None, ("dp", "tensor")),
        check_vma=False,
    )
```

profile of v0, /device:TPU:0, one launch (start us, length us, event | category | flops | bytes accessed | tf_op | source)
XLA Modules:
  0.0 210.4 jit_solution(1678884307394974821)
XLA Ops:
  6.5 0.0 copy-start
  6.5 0.0 copy-start.1
  6.5 0.0 all-reduce.2.cloned.1.call-start
  6.5 6.2 %fusion.11 = f32[4096,64]{0,1:T(8,128)S(1)} fusion(bf16[4096,1024]{1,0:T(8,128)(2,1)} %param.7, bf16[1024,64]{0,1:T(8,128)(2,1)} %param.9), kind=kOutput, calls=%fused_computation.15 | convolution fusion | flops 536870912 | bytes 9568256 | tf_op jit(solution)/shard_map/dot_general | solution.py:25
  12.7 0.0 copy-done.1
  12.7 14.2 %fusion.10 = f32[4096,64]{0,1:T(8,128)S(1)} fusion(bf16[4096,3584]{1,0:T(8,128)(2,1)} %param.6, bf16[3584,64]{0,1:T(8,128)(2,1)S(1)} %copy-done.1), kind=kOutput, calls=%fused_computation.14 | convolution fusion | flops 1879048192 | bytes 30867456 | tf_op jit(solution)/shard_map/dot_general | solution.py:24
  26.9 1.4 pad_maximum_fusion
  28.3 0.0 copy-start.2
  28.3 0.0 all-reduce.2.cloned.1.call-update
  28.4 0.0 reduce-scatter.2.cloned.1.call-start
  28.4 0.6 copy-done.2
  29.0 0.1 copy.8
  29.1 0.1 reduce
  29.3 0.1 convert_bitcast_fusion
  29.4 104.2 %all-reduce.2.cloned.1.call-done = f32[4096,128]{0,1:T(8,128)} async-done(((f32[4096,128]{0,1:T(8,128)}), f32[4096,128]{0,1:T(8,128)}) %all-reduce.2.cloned.1.call-update) | async-done | bytes 2097168 | tf_op jit(solution)/shard_map/psum | solution.py:33
  133.6 0.0 slice-start
  133.6 1.2 slice-done
  134.8 3.0 %fusion.2 = f32[16,8,64]{2,0,1:T(8,128)S(1)} fusion(f32[4096,128]{0,1:T(8,128)} %all-reduce.2.cloned.1.call-done, f32[4096,16]{0,1:T(8,128)S(1)} %convert_bitcast_fusion, f32[4096,8]{0,1:T(8,128)S(1)} %constant_dynamic-slice_fusion), kind=kOutput, calls=%fused_computation.3 | convolution fusion | flops 403177472 | bytes 1474560 | tf_op jit(solution)/shard_map/pt,ti,tj->pij/dot_general | solution.py:15
  137.8 0.1 reshape.34
  137.9 10.6 %psum.15 = f32[16,512]{1,0:T(8,128)S(1)} all-reduce(f32[16,512]{1,0:T(8,128)S(1)} %reshape.34), channel_id=1, replica_groups=mesh['dp'=4,'tensor'=8] {'dp'}, use_global_device_ids=true, to_apply=%region_2.3 | all-reduce | flops 8192 | bytes 65536 | tf_op jit(solution)/shard_map/psum | solution.py:42
  148.6 0.0 copy-done
  148.6 1.0 fusion.7
  149.6 0.0 reduce-scatter.2.cloned.1.call-update
  149.6 54.0 %reduce-scatter.2.cloned.1.call-done = f32[16,128]{1,0:T(8,128)} async-done(((f32[16,1024]{1,0:T(8,128)}), f32[16,128]{1,0:T(8,128)}) %reduce-scatter.2.cloned.1.call-update) | async-done | bytes 8208 | tf_op jit(solution)/shard_map/reduce_scatter | solution.py:47
  (5 shorter events, 0.1 us)
Async XLA Ops:
  6.5 142.0 %copy-start = (bf16[1024,512]{1,0:T(8,128)(2,1)S(1)}, bf16[1024,512]{1,0:T(8,128)(2,1)}, u32[]{:S(2)}) copy-start(bf16[1024,512]{1,0:T(8,128)(2,1)} %param.11) | copy-start | bytes 3145732
  6.5 6.2 %copy-start.1 = (bf16[3584,64]{0,1:T(8,128)(2,1)S(1)}, bf16[3584,64]{0,1:T(8,128)(2,1)}, u32[]{:S(2)}) copy-start(bf16[3584,64]{0,1:T(8,128)(2,1)} %param.8) | copy-start | bytes 1376260
  6.5 127.0 %all-reduce.2.cloned.1.call-start = ((), (), s32[]{:S(2)}) async-start(), calls=%async_computation.1 | async-start | bytes 4194304 | tf_op jit(solution)/shard_map/psum | solution.py:33
  28.3 0.7 copy-start.2
  28.4 175.2 %reduce-scatter.2.cloned.1.call-start = ((), (), s32[]{:S(2)}) async-start(), calls=%async_computation.2 | async-start | bytes 73728 | tf_op jit(solution)/shard_map/reduce_scatter | solution.py:47
  133.6 1.2 slice-start
Sparse Core Ops, SparseCore 0:
  28.5 105.0 all-reduce.1
  149.7 53.7 reduce-scatter.1
where the time goes:
time: 211 us; the launch traced here: 210 us
  waiting for transfers between devices  158 us (75%)
  matrix products  24.4 us (12%)
  between operations  13.5 us (6%)
  blocking collectives  10.6 us (5%)
    psum x1, waiting for transfers between devices, shards(): summed_pair = lax.psum(paired, 'tensor')  104 us
    reduce_scatter x1, waiting for transfers between devices, shards(): lax.psum_scatter(partial_value, 'tensor', scatter_dimension=1, tiled=True)  54 us
    dot_general x1, matrix products, shards(): act_part = jnp.dot(inputs, proj_in, preferred_element_type=jnp.float32)  14.2 us
    psum x1, blocking collectives, shards(): summed = lax.psum(gram_rows, 'dp')  10.6 us
    dot_general x1, matrix products, shards(): grad_part = jnp.dot(out_grads, proj_out, preferred_element_type=jnp.float32)  6.15 us
  transfers between devices with their start and end apart: 2, of which 2 were waited for; matrix products, arithmetic and copies ran while one was open for 0% of the time, Pallas kernels for 0%

commit v1 on v0

--- a/solution.py
+++ b/solution.py
@@ -2,6 +2,16 @@
 import jax.numpy as jnp
 from jax import lax
 from jax.sharding import PartitionSpec as P
+
+
+def _treat_cycles(array_here, shard_axis):
+    num = jax.lax.axis_size(shard_axis)
+    state_next = array_here
+    for idx in [at for at in (1, 2, 4, 8, 16) if at < num]:
+        state_next = state_next + jax.lax.ppermute(
+            state_next, axis_name=shard_axis, perm=[(c, c ^ idx) for c in range(num)]
+        )
+    return state_next
 
 
 def member_rows(positions, prompt_starts, prompt_ends):
@@ -30,7 +40,7 @@
     tensor_pos = lax.axis_index("tensor")
     slice_width = proj_rank * proj_rank // tensor_count
     first_row = lax.axis_index("dp") * tok_rows
-    summed_pair = lax.psum(paired, "tensor")
+    summed_pair = _treat_cycles(paired, "tensor")
     row_count = proj_rank // tensor_count
     grad_rows = lax.dynamic_slice_in_dim(
         summed_pair[:, proj_rank:], tensor_pos * row_count, row_count, 1

time: 211 us -> 290 us (1.37)
  waiting for transfers between devices: 158 us -> 236 us
  starting transfers between devices: 0.04 us -> 7.55 us
  matrix products: 24.4 us -> 19.8 us
    ppermute x0 -> x3, waiting for transfers between devices: none -> 180 us  [_treat_cycles(): jax.lax.ppermute(state_next, axis_name=shard_axis, perm=[(c, c ^ idx) for...]
    psum x1 -> x0, waiting for transfers between devices: 104 us -> none  [shards(): summed_pair = lax.psum(paired, 'tensor')]
    ppermute x0 -> x3, starting transfers between devices: none -> 7.55 us  [_treat_cycles(): jax.lax.ppermute(state_next, axis_name=shard_axis, perm=[(c, c ^ idx) for...]
    dot_general x1, matrix products: 6.15 us -> 2.66 us  [shards(): grad_part = jnp.dot(out_grads, proj_out, preferred_element_type=jnp.float32)]
  transfers between devices with their start and end apart: 2 -> 4, of which waited for: 2 -> 4; matrix products, arithmetic and copies ran while one was open for 0% -> 0% of each run, Pallas kernels for 0% -> 0%
where the time goes in v1:
time: 290 us
  waiting for transfers between devices  236 us (81%)
  matrix products  19.8 us (7%)
  between operations  13.5 us (5%)
  blocking collectives  10.3 us (4%)
  starting transfers between devices  7.55 us (3%)
    ppermute x3, waiting for transfers between devices, _treat_cycles(): jax.lax.ppermute(state_next, axis_name=shard_axis, perm=[(c, c ^ idx) for...  180 us
    reduce_scatter x1, waiting for transfers between devices, shards(): lax.psum_scatter(partial_value, 'tensor', scatter_dimension=1, tiled=True)  56 us
    dot_general x1, matrix products, shards(): act_part = jnp.dot(inputs, proj_in, preferred_element_type=jnp.float32)  14.4 us
    psum x1, blocking collectives, shards(): summed = lax.psum(gram_rows, 'dp')  10.3 us
    ppermute x3, starting transfers between devices, _treat_cycles(): jax.lax.ppermute(state_next, axis_name=shard_axis, perm=[(c, c ^ idx) for...  7.55 us
  transfers between devices with their start and end apart: 4, of which 4 were waited for; matrix products, arithmetic and copies ran while one was open for 0% of the time, Pallas kernels for 0%

profile of v1, /device:TPU:0, one launch (start us, length us, event | category | flops | bytes accessed | tf_op | source)
XLA Modules:
  0.0 289.7 jit_solution(18234952908170459080)
XLA Ops:
  6.5 0.0 copy-start
  6.5 0.0 copy-start.2
  6.5 0.0 reduce-scatter.2.cloned.1.call-start
  6.5 0.0 copy-start.1
  6.5 14.4 %fusion.11 = f32[4096,64]{0,1:T(8,128)S(1)} fusion(bf16[4096,3584]{1,0:T(8,128)(2,1)} %param.6, bf16[3584,64]{0,1:T(8,128)(2,1)} %param.8), kind=kOutput, calls=%fused_computation.15 | convolution fusion | flops 1879048192 | bytes 30867456 | tf_op jit(solution)/shard_map/dot_general | solution.py:34
  20.9 0.0 copy-done.2
  20.9 0.0 copy-done.1
  20.9 2.7 fusion.12
  23.6 0.2 pad_maximum_fusion
  23.8 3.0 %collective-permute-start = (f32[4096,128]{0,1:T(8,128)S(1)}, f32[4096,128]{0,1:T(8,128)S(1)}, u32[]{:S(2)}, u32[]{:S(2)}) collective-permute-start(f32[4096,128]{0,1:T(8,128)S(1)} %pad_maximum_fusion), channel_id=1, source_target_pairs={{0,1},{1,0},{2,3},{3,2},{4,5},{5,4},{6,7},{7,6},{8,9},{9,8},{10,11... | collective-permute-start | bytes 6291464 | tf_op jit(solution)/shard_map/ppermute | solution.py:11
  26.8 45.6 %collective-permute-done = f32[4096,128]{0,1:T(8,128)S(1)} collective-permute-done((f32[4096,128]{0,1:T(8,128)S(1)}, f32[4096,128]{0,1:T(8,128)S(1)}, u32[]{:S(2)}, u32[]{:S(2)}) %collective-permute-start) | collective-permute-done | bytes 2097184 | tf_op jit(solution)/shard_map/ppermute | solution.py:11
  72.4 0.2 fusion.9
  72.7 0.0 copy-start.3
  72.7 1.9 collective-permute-start.1
  74.6 45.0 %collective-permute-done.1 = f32[4096,128]{0,1:T(8,128)S(1)} collective-permute-done((f32[4096,128]{0,1:T(8,128)S(1)}, f32[4096,128]{0,1:T(8,128)S(1)}, u32[]{:S(2)}, u32[]{:S(2)}) %collective-permute-start.1) | collective-permute-done | bytes 2097184 | tf_op jit(solution)/shard_map/ppermute | solution.py:11
  119.5 0.2 add.27
  119.8 2.6 collective-permute-start.2
  122.4 0.0 copy-done.3
  122.4 0.1 copy.8
  122.5 0.1 reduce
  122.7 0.1 convert_bitcast_fusion
  122.8 88.9 %collective-permute-done.2 = f32[4096,128]{0,1:T(8,128)} collective-permute-done((f32[4096,128]{0,1:T(8,128)S(1)}, f32[4096,128]{0,1:T(8,128)}, u32[]{:S(2)}, u32[]{:S(2)}) %collective-permute-start.2) | collective-permute-done | bytes 2097184 | tf_op jit(solution)/shard_map/ppermute | solution.py:11
  211.7 1.8 add.28
  213.5 0.1 slice.8
  213.6 1.8 fusion.2
  215.5 0.1 reshape.34
  215.5 10.3 %psum.7 = f32[16,512]{1,0:T(8,128)S(1)} all-reduce(f32[16,512]{1,0:T(8,128)S(1)} %reshape.34), channel_id=1, replica_groups=mesh['dp'=4,'tensor'=8] {'dp'}, use_global_device_ids=true, to_apply=%region_1.2 | all-reduce | flops 8192 | bytes 65536 | tf_op jit(solution)/shard_map/psum | solution.py:52
  225.8 0.0 copy-done
  225.8 1.0 fusion.7
  226.8 0.0 reduce-scatter.2.cloned.1.call-update
  226.9 56.0 %reduce-scatter.2.cloned.1.call-done = f32[16,128]{1,0:T(8,128)} async-done(((f32[16,1024]{1,0:T(8,128)}), f32[16,128]{1,0:T(8,128)}) %reduce-scatter.2.cloned.1.call-update) | async-done | bytes 8208 | tf_op jit(solution)/shard_map/reduce_scatter | solution.py:57
  (5 shorter events, 0.1 us)
Async XLA Ops:
  6.5 219.3 %copy-start = (bf16[1024,512]{1,0:T(8,128)(2,1)S(1)}, bf16[1024,512]{1,0:T(8,128)(2,1)}, u32[]{:S(2)}) copy-start(bf16[1024,512]{1,0:T(8,128)(2,1)} %param.11) | copy-start | bytes 3145732
  6.5 14.4 %copy-start.2 = (bf16[1024,64]{0,1:T(8,128)(2,1)S(1)}, bf16[1024,64]{0,1:T(8,128)(2,1)}, u32[]{:S(2)}) copy-start(bf16[1024,64]{0,1:T(8,128)(2,1)} %param.9) | copy-start | bytes 393220
  6.5 276.3 %reduce-scatter.2.cloned.1.call-start = ((), (), s32[]{:S(2)}) async-start(), calls=%async_computation.1 | async-start | bytes 73728 | tf_op jit(solution)/shard_map/reduce_scatter | solution.py:57
  6.5 14.4 %copy-start.1 = (bf16[4096,1024]{1,0:T(8,128)(2,1)S(1)}, bf16[4096,1024]{1,0:T(8,128)(2,1)}, u32[]{:S(2)}) copy-start(bf16[4096,1024]{1,0:T(8,128)(2,1)} %param.7) | copy-start | bytes 25165828
  23.8 48.7 %collective-permute-start = (f32[4096,128]{0,1:T(8,128)S(1)}, f32[4096,128]{0,1:T(8,128)S(1)}, u32[]{:S(2)}, u32[]{:S(2)}) collective-permute-start(f32[4096,128]{0,1:T(8,128)S(1)} %pad_maximum_fusion), channel_id=1, source_target_pairs={{0,1},{1,0},{2,3},{3,2},{4,5},{5,4},{6,7},{7,6},{8,9},{9,8},{10,11... | collective-permute-start | bytes 6291464 | tf_op jit(solution)/shard_map/ppermute | solution.py:11
  72.7 49.7 %copy-start.3 = (s32[16]{0:T(128)S(1)}, s32[16]{0:T(128)}, u32[]{:S(2)}) copy-start(s32[16]{0:T(128)} %param.10) | copy-start | bytes 196
  72.7 46.9 %collective-permute-start.1 = (f32[4096,128]{0,1:T(8,128)S(1)}, f32[4096,128]{0,1:T(8,128)S(1)}, u32[]{:S(2)}, u32[]{:S(2)}) collective-permute-start(f32[4096,128]{0,1:T(8,128)S(1)} %fusion.9), channel_id=1, source_target_pairs={{0,2},{1,3},{2,0},{3,1},{4,6},{5,7},{6,4},{7,5},{8,10},{9,11},{10,... | collective-permute-start | bytes 6291464 | tf_op jit(solution)/shard_map/ppermute | solution.py:11
  119.8 91.9 %collective-permute-start.2 = (f32[4096,128]{0,1:T(8,128)S(1)}, f32[4096,128]{0,1:T(8,128)}, u32[]{:S(2)}, u32[]{:S(2)}) collective-permute-start(f32[4096,128]{0,1:T(8,128)S(1)} %add.27), channel_id=1, source_target_pairs={{0,4},{1,5},{2,6},{3,7},{4,0},{5,1},{6,2},{7,3},{8,12},{9,13},{10,... | collective-permute-start | bytes 6291464 | tf_op jit(solution)/shard_map/ppermute | solution.py:11
Sparse Core Ops, SparseCore 0:
  227.0 55.7 reduce-scatter.1
